TPU v7x, 32 devices: a whole 2x2x4 slice. The times are simulated.
32 devices in a mesh: rep: 2 (over y), blk: 16 (over z, x, core).
Axes of the slice: x: 2, y: 2, z: 4, core: 2. Of those that a mesh axis runs over, the one named last changes fastest.
Arguments:
- a_blocks: float32 [16, 48, 256, 256], P('blk', 'rep'), may hold values from -0.375 to 0.375
- a_rows: int32 [16, 48], P('blk', 'rep'), may hold values from 0 to 31, as said below
- a_cols: int32 [16, 48], P('blk', 'rep'), may hold values from 0 to 31, as said below
- b_blocks: float32 [16, 6, 256, 256], P('blk'), may hold values from -6 to 6
- b_rows: int32 [16, 6], P('blk'), may hold values from 0 to 31, as said below
- b_cols: int32 [16, 6], P('blk'), may hold values from 0 to 31
- b_count: int32 [16], P('blk'), may hold values from 1 to 6, as said below
- c_rows: int32 [16, 16], P('blk'), may hold values from 0 to 31, as said below
- c_cols: int32 [16, 16], P('blk'), may hold values from 0 to 31
Outputs:
- iterate: float32 [16, 16, 256, 256], P('blk', 'rep')
Inputs may be any that keep to these rules, and one draw needn't show every extreme that they name: `a_rows`: entry [d, g] lies in the block rows d * 2 to d * 2 + 1. `a_cols`: entry [d, r * 6 * 4 + k * 4 + m] (m < 4) lies in the block rows e * 2 to e * 2 + 1 with e = (d + (r - 1) * 6 + k) modulo the size of blk. `b_rows`: entry [e, q] lies in the block rows e * 2 to e * 2 + 1. `b_count`: equals 6 on at least one index. `c_rows`: entry [d, t] lies in the block rows d * 2 to d * 2 + 1.
All inputs are finite; a program needn't handle non-finite values.
Results may differ from a plain program's by a relative error of at most 0.0003.
Values sent between devices are 32-bit elements; how exact they have to be, the bound alone decides.
A program may use at most 128 MiB of HBM per device.

v0:
```python
import jax
import jax.numpy as jnp
from jax import lax
from jax.sharding import PartitionSpec as P

STEPS = 6
PANEL = 6
A_SLOTS = 4


def shifted(block, axis, distance):
    devices = range(lax.axis_size(axis))
    route = [((i - distance) % len(devices), i) for i in devices]
    return lax.ppermute(block, axis, route)


def contribute(
    partial_sum, a_group, row_group, col_group, blocks, rows, cols, count, target_rows, target_cols
):
    products = jnp.einsum("kij,qjl->kqil", a_group, blocks, precision=lax.Precision.HIGHEST)
    slot_index = jnp.arange(blocks.shape[0], dtype=jnp.int32)
    live = slot_index < count
    weights = (
        (row_group[None, :, None] == target_rows[:, None, None])
        & (col_group[None, :, None] == rows[None, None, :])
        & (cols[None, None, :] == target_cols[:, None, None])
        & live[None, None, :]
    )
    return partial_sum + jnp.einsum(
        "tkq,kqil->til", weights.astype(jnp.float32), products, precision=lax.Precision.HIGHEST
    )


def local(a_blocks, a_rows, a_cols, b_blocks, b_rows, b_cols, b_count, c_rows, c_cols):
    replica = lax.axis_index("rep")
    own_panel = (b_blocks[0], b_rows[0], b_cols[0], b_count)
    target_rows = c_rows[0]
    target_cols = c_cols[0]
    block = a_blocks.shape[-1]
    partial_sum = jnp.zeros((target_rows.shape[0], block, block), jnp.float32)
    panel = PANEL
    skewed = shifted((own_panel[0], own_panel[1], own_panel[2], own_panel[3]), "blk", STEPS)
    current = tuple(
        (jnp.where(replica == 0, moved, mine) for moved, mine in zip(skewed, own_panel))
    )
    stacked = current
    have = 1
    while have < STEPS:
        take = min(have, STEPS - have)
        arrived = shifted(
            (
                stacked[0][: take * panel],
                stacked[1][: take * panel],
                stacked[2][: take * panel],
                stacked[3][:take],
            ),
            "blk",
            -have,
        )
        stacked = tuple(
            (jnp.concatenate([earlier, later]) for earlier, later in zip(stacked, arrived))
        )
        have = have + take
    for index in range(STEPS):
        start = index * A_SLOTS
        a_group = a_blocks[0, start : start + A_SLOTS]
        row_group = a_rows[0, start : start + A_SLOTS]
        col_group = a_cols[0, start : start + A_SLOTS]
        lower = index * panel
        partial_sum = contribute(
            partial_sum,
            a_group,
            row_group,
            col_group,
            stacked[0][lower : lower + panel],
            stacked[1][lower : lower + panel],
            stacked[2][lower : lower + panel],
            stacked[3][index],
            target_rows,
            target_cols,
        )
    summed = lax.psum_scatter(partial_sum, "rep", scatter_dimension=0, tiled=True)
    half = summed.shape[0]
    rows_half = lax.dynamic_slice_in_dim(target_rows, replica * half, half)
    cols_half = lax.dynamic_slice_in_dim(target_cols, replica * half, half)
    diagonal = (rows_half == cols_half).astype(jnp.float32)
    identity = jnp.eye(block, dtype=jnp.float32)
    result = 1.5 * diagonal[:, None, None] * identity[None, :, :] - 0.5 * summed
    return result[None]


def solution(mesh):
    return jax.shard_map(
        local,
        mesh=mesh,
        in_specs=(
            P("blk", "rep", None, None),
            P("blk", "rep"),
            P("blk", "rep"),
            P("blk", None, None, None),
            P("blk", None),
            P("blk", None),
            P("blk"),
            P("blk", None),
            P("blk", None),
        ),
        out_specs=P("blk", "rep", None, None),
        check_vma=False,
    )
```

profile of v0, /device:TPU:3, one launch (start us, length us, event | category | flops | bytes accessed | tf_op | source)
XLA Modules:
  0.0 424.2 jit_solution(4695772045869825205)
XLA Ops:
  6.5 2.3 collective-permute-start.3
  8.8 2.2 collective-permute-start.1
  11.1 2.2 collective-permute-start.2
  14.0 0.9 slice_bitcast_fusion.18
  14.9 0.9 slice_bitcast_fusion.19
  15.9 0.7 broadcast_compare_fusion.17
  16.6 28.1 %collective-permute-done.2 = s32[1]{0:T(128)} collective-permute-done((s32[1]{0:T(128)}, s32[1]{0:T(128)}, u32[]{:S(2)}, u32[]{:S(2)}) %collective-permute-start.2) | collective-permute-done | bytes 36 | tf_op jit(solution)/shard_map/ppermute | solution.py:14
  45.3 2.7 collective-permute-start.6
  48.0 1.2 collective-permute-done.6
  49.2 0.6 pad_add_fusion.2
  49.8 35.0 %collective-permute-start.14 = (s32[2]{0:T(128)S(1)}, s32[2]{0:T(128)S(1)}, u32[]{:S(2)}, u32[]{:S(2)}) collective-permute-start(s32[2]{0:T(128)S(1)} %pad_add_fusion.2), channel_id=1, source_target_pairs={{4,0},{5,1},{6,2},{7,3},{8,4},{9,5},{10,6},{11,7},{12,8},{13,9},{1... | collective-permute-start | bytes 32 | tf_op jit(solution)/shard_map/ppermute | solution.py:14
  84.9 1.4 collective-permute-start.10
  86.3 1.6 broadcast_select_fusion
  88.5 0.6 fusion.89
  89.8 0.6 fusion.86
  90.4 0.6 iota_compare_fusion.3
  91.6 0.7 iota_compare_fusion.1
  92.3 1.6 collective-permute-start.5
  94.1 14.7 %collective-permute-done.5 = s32[6]{0:T(128)S(1)} collective-permute-done((s32[6]{0:T(128)S(1)}, s32[6]{0:T(128)S(1)}, u32[]{:S(2)}, u32[]{:S(2)}) %collective-permute-start.5) | collective-permute-done | bytes 56 | tf_op jit(solution)/shard_map/ppermute | solution.py:14
  109.2 1.6 collective-permute-start.13
  110.9 1.2 collective-permute-start.8
  112.0 1.9 pad_maximum_fusion
  114.0 1.9 collective-permute-start.15
  116.0 0.8 collective-permute-start.11
  117.3 13.7 %fusion.20 = f32[6,256,4,256]{3,1,2,0:T(8,128)} fusion(f32[6,256,256]{2,1,0:T(8,128)S(1)} %broadcast_select_fusion, f32[1,24,256,256]{3,2,1,0:T(8,128)} %param.9), kind=kOutput, calls=%fused_computation.29 | convolution fusion | flops 4831838208 | bytes 8912896 | tf_op jit(solution)/shard_map/kij,qjl->kqil/dot_general | solution.py:20
  131.0 9.7 %copy.12 = f32[6,256,4,256]{1,0,2,3:T(8,128)} copy(f32[6,256,4,256]{3,1,2,0:T(8,128)} %fusion.20) | data formatting | bytes 12582912 | tf_op jit(solution)/shard_map/kij,qjl->kqil/dot_general | solution.py:20
  140.7 13.4 %fusion.18 = f32[6,256,4,256]{3,1,2,0:T(8,128)} fusion(f32[6,256,256]{2,1,0:T(8,128)S(1)} %collective-permute-done.7, f32[1,24,256,256]{3,2,1,0:T(8,128)} %param.9), kind=kOutput, calls=%fused_computation.27 | convolution fusion | flops 4831838208 | bytes 8912896 | tf_op jit(solution)/shard_map/kij,qjl->kqil/dot_general | solution.py:20
  154.0 9.6 %copy.15 = f32[6,256,4,256]{1,0,2,3:T(8,128)} copy(f32[6,256,4,256]{3,1,2,0:T(8,128)} %fusion.18) | data formatting | bytes 12582912 | tf_op jit(solution)/shard_map/kij,qjl->kqil/dot_general | solution.py:20
  163.6 7.9 %fusion.8 = f32[16,256,256,1]{2,0,3,1:T(8,128)} fusion(f32[6,256,4,256]{1,0,2,3:T(8,128)} %copy.15, pred[6]{0:T(512)(128)(4,1)S(1)} %iota_compare_fusion.5, pred[16,6]{0,1:T(8,128)(4,1)S(1)} %get-tuple-element.24, pred[4,6]{1,0:T(4,128)(4,1)S(1)} %broadcast_compare_fusion.10, pred[16,4]{0,1:T(4,128)(4,1)S(1)} %get-tuple-element.6), kind=kOutput, calls=%fused_computation.8 | convolution fusion | flops 301991040 | bytes 10485950 | tf_op jit(solution)/shard_map/tkq,kqil->til/dot_general | solution.py:29
  171.6 12.2 %collective-permute-done.15 = f32[12,256,256]{2,1,0:T(8,128)} collective-permute-done((f32[12,256,256]{2,1,0:T(8,128)}, f32[12,256,256]{2,1,0:T(8,128)}, u32[]{:S(2)}, u32[]{:S(2)}) %collective-permute-start.15) | collective-permute-done | bytes 3145760 | tf_op jit(solution)/shard_map/ppermute | solution.py:14
  183.8 13.3 %fusion.15 = f32[6,256,4,256]{3,1,2,0:T(8,128)} fusion(f32[12,256,256]{2,1,0:T(8,128)} %collective-permute-done.15, f32[1,24,256,256]{3,2,1,0:T(8,128)} %param.9), kind=kOutput, calls=%fused_computation.22 | convolution fusion | flops 4831838208 | bytes 8912896 | tf_op jit(solution)/shard_map/kij,qjl->kqil/dot_general | solution.py:20
  197.2 9.6 %copy.24 = f32[6,256,4,256]{1,0,2,3:T(8,128)} copy(f32[6,256,4,256]{3,1,2,0:T(8,128)} %fusion.15) | data formatting | bytes 12582912 | tf_op jit(solution)/shard_map/kij,qjl->kqil/dot_general | solution.py:20
  206.8 44.1 %collective-permute-done.11 = f32[12,256,256]{2,1,0:T(8,128)} collective-permute-done((f32[12,256,256]{2,1,0:T(8,128)}, f32[12,256,256]{2,1,0:T(8,128)}, u32[]{:S(2)}, u32[]{:S(2)}) %collective-permute-start.11) | collective-permute-done | bytes 3145760 | tf_op jit(solution)/shard_map/ppermute | solution.py:14
  250.9 13.5 %fusion.16 = f32[6,256,4,256]{3,1,2,0:T(8,128)} fusion(f32[12,256,256]{2,1,0:T(8,128)} %collective-permute-done.11, f32[1,24,256,256]{3,2,1,0:T(8,128)} %param.9), kind=kOutput, calls=%fused_computation.24 | convolution fusion | flops 4831838208 | bytes 8912896 | tf_op jit(solution)/shard_map/kij,qjl->kqil/dot_general | solution.py:20
  264.4 9.7 %copy.21 = f32[6,256,4,256]{1,0,2,3:T(8,128)} copy(f32[6,256,4,256]{3,1,2,0:T(8,128)} %fusion.16) | data formatting | bytes 12582912 | tf_op jit(solution)/shard_map/kij,qjl->kqil/dot_general | solution.py:20
  274.1 13.3 %fusion.17 = f32[6,256,4,256]{3,1,2,0:T(8,128)} fusion(f32[12,256,256]{2,1,0:T(8,128)} %collective-permute-done.11, f32[1,24,256,256]{3,2,1,0:T(8,128)} %param.9), kind=kOutput, calls=%fused_computation.26 | convolution fusion | flops 4831838208 | bytes 8912896 | tf_op jit(solution)/shard_map/kij,qjl->kqil/dot_general | solution.py:20
  287.4 9.7 %copy.18 = f32[6,256,4,256]{1,0,2,3:T(8,128)} copy(f32[6,256,4,256]{3,1,2,0:T(8,128)} %fusion.17) | data formatting | bytes 12582912 | tf_op jit(solution)/shard_map/kij,qjl->kqil/dot_general | solution.py:20
  297.1 13.6 %fusion.14 = f32[6,256,4,256]{3,1,2,0:T(8,128)} fusion(f32[12,256,256]{2,1,0:T(8,128)} %collective-permute-done.15, f32[1,24,256,256]{3,2,1,0:T(8,128)} %param.9), kind=kOutput, calls=%fused_computation.20 | convolution fusion | flops 4831838208 | bytes 8912896 | tf_op jit(solution)/shard_map/kij,qjl->kqil/dot_general | solution.py:20
  310.7 9.7 %copy.27 = f32[6,256,4,256]{1,0,2,3:T(8,128)} copy(f32[6,256,4,256]{3,1,2,0:T(8,128)} %fusion.14) | data formatting | bytes 12582912 | tf_op jit(solution)/shard_map/kij,qjl->kqil/dot_general | solution.py:20
  320.4 6.7 %fusion.2 = f32[16,256,256,1]{2,0,3,1:T(8,128)S(1)} fusion(f32[6,256,4,256]{1,0,2,3:T(8,128)} %copy.24, pred[6]{0:T(512)(128)(4,1)S(1)} %iota_compare_fusion.2, pred[16,6]{0,1:T(8,128)(4,1)S(1)} %get-tuple-element.27, pred[4,6]{1,0:T(4,128)(4,1)S(1)} %get-tuple-element.42, pred[16,4]{0,1:T(4,128)(4,1)S(1)} %get-tuple-element.9), kind=kOutput, calls=%fused_computation.2 | convolution fusion | flops 301991040 | bytes 10485950 | tf_op jit(solution)/shard_map/tkq,kqil->til/dot_general | solution.py:29
  327.1 7.9 %fusion.4 = f32[16,256,256,1]{2,0,3,1:T(8,128)} fusion(f32[6,256,4,256]{1,0,2,3:T(8,128)} %copy.21, pred[6]{0:T(512)(128)(4,1)S(1)} %iota_compare_fusion.3, pred[16,6]{0,1:T(8,128)(4,1)S(1)} %get-tuple-element.26, pred[4,6]{1,0:T(4,128)(4,1)S(1)} %get-tuple-element.43, pred[16,4]{0,1:T(4,128)(4,1)S(1)} %get-tuple-element.8), kind=kOutput, calls=%fused_computation.4 | convolution fusion | flops 301991040 | bytes 10485950 | tf_op jit(solution)/shard_map/tkq,kqil->til/dot_general | solution.py:29
  335.0 5.7 %fusion.6 = f32[16,256,256,1]{2,0,3,1:T(8,128)} fusion(f32[6,256,4,256]{1,0,2,3:T(8,128)S(1)} %bitcast.166, pred[6]{0:T(512)(128)(4,1)S(1)} %iota_compare_fusion.4, pred[16,6]{0,1:T(8,128)(4,1)S(1)} %get-tuple-element.25, pred[4,6]{1,0:T(4,128)(4,1)S(1)} %get-tuple-element.44, pred[16,4]{0,1:T(4,128)(4,1)S(1)} %get-tuple-element.7), kind=kOutput, calls=%fused_computation.6 | convolution fusion | flops 301991040 | bytes 10485950 | tf_op jit(solution)/shard_map/tkq,kqil->til/dot_general | solution.py:29
  340.7 5.9 %fusion = f32[16,256,256,1]{2,0,3,1:T(8,128)} fusion(f32[6,256,4,256]{1,0,2,3:T(8,128)S(1)} %bitcast.164, pred[6]{0:T(512)(128)(4,1)S(1)} %iota_compare_fusion.1, pred[16,6]{0,1:T(8,128)(4,1)S(1)} %get-tuple-element.28, pred[4,6]{1,0:T(4,128)(4,1)S(1)} %get-tuple-element.41, pred[16,4]{0,1:T(4,128)(4,1)S(1)} %get-tuple-element.10), kind=kOutput, calls=%fused_computation | convolution fusion | flops 301991040 | bytes 10485950 | tf_op jit(solution)/shard_map/tkq,kqil->til/dot_general | solution.py:29
  346.6 9.7 %bitcast_add_fusion = f32[16,256,256]{2,0,1:T(8,128)} fusion(f32[16,256,256,1]{2,0,3,1:T(8,128)} %fusion, f32[16,256,256,1]{2,0,3,1:T(8,128)S(1)} %fusion.2, f32[16,256,256,1]{2,0,3,1:T(8,128)} %fusion.4, f32[16,256,256,1]{2,0,3,1:T(8,128)} %fusion.6, f32[16,256,256,1]{2,0,3,1:T(8,128)S(1)} %copy-done, f32[6,256,4,256]{1,0,2,3:T(8,128)S(1)} %bitcast.162, ...), kind=kOutput, calls=%fused_computation.12 | convolution fusion | flops 307233920 | bytes 31457470 | tf_op jit(solution)/shard_map/tkq,kqil->til/dot_general | solution.py:29
  356.4 0.6 copy-done.2
  357.1 55.9 %reduce-scatter.2.cloned.1.call-done = f32[8,256,256]{2,0,1:T(8,128)} async-done(((f32[16,256,256]{2,0,1:T(8,128)}), f32[8,256,256]{2,0,1:T(8,128)}) %reduce-scatter.2.cloned.1.call-update) | async-done | bytes 2097168 | tf_op jit(solution)/shard_map/reduce_scatter | solution.py:82
  413.0 1.9 subtract_bitcast_fusion
  414.9 2.0 copy.10
  (61 shorter events, 3.2 us)
Async XLA Ops:
  6.5 85.8 %copy-start.3 = (s32[1,6]{1,0:T(1,128)S(1)}, s32[1,6]{1,0:T(1,128)}, u32[]{:S(2)}) copy-start(s32[1,6]{1,0:T(1,128)} %param.14) | copy-start | bytes 76
  6.5 87.4 %copy-start.4 = (s32[1,6]{1,0:T(1,128)S(1)}, s32[1,6]{1,0:T(1,128)}, u32[]{:S(2)}) copy-start(s32[1,6]{1,0:T(1,128)} %param.13) | copy-start | bytes 76
  6.5 406.5 %reduce-scatter.2.cloned.1.call-start = ((), (), s32[]{:S(2)}) async-start(), calls=%async_computation.1 | async-start | bytes 6291456 | tf_op jit(solution)/shard_map/reduce_scatter | solution.py:82
  6.5 79.7 %collective-permute-start.3 = (f32[6,256,256]{2,1,0:T(8,128)}, f32[6,256,256]{2,1,0:T(8,128)S(1)}, u32[]{:S(2)}, u32[]{:S(2)}) collective-permute-start(f32[6,256,256]{2,1,0:T(8,128)} %bitcast.167), channel_id=1, source_target_pairs={{10,0},{11,1},{12,2},{13,3},{14,4},{15,5},{0,6},{1,7},{2,8},{3,9},... | collective-permute-start | bytes 4718600 | tf_op jit(solution)/shard_map/ppermute | solution.py:14
  8.8 83.5 %collective-permute-start.1 = (s32[6]{0:T(128)}, s32[6]{0:T(128)S(1)}, u32[]{:S(2)}, u32[]{:S(2)}) collective-permute-start(s32[6]{0:T(128)} %bitcast.170), channel_id=1, source_target_pairs={{10,0},{11,1},{12,2},{13,3},{14,4},{15,5},{0,6},{1,7},{2,8},{3,9},... | collective-permute-start | bytes 80 | tf_op jit(solution)/shard_map/ppermute | solution.py:14
  11.0 82.9 %collective-permute-start = (s32[6]{0:T(128)}, s32[6]{0:T(128)S(1)}, u32[]{:S(2)}, u32[]{:S(2)}) collective-permute-start(s32[6]{0:T(128)} %bitcast.171), channel_id=1, source_target_pairs={{10,0},{11,1},{12,2},{13,3},{14,4},{15,5},{0,6},{1,7},{2,8},{3,9},... | collective-permute-start | bytes 80 | tf_op jit(solution)/shard_map/ppermute | solution.py:14
  11.1 33.7 %collective-permute-start.2 = (s32[1]{0:T(128)}, s32[1]{0:T(128)}, u32[]{:S(2)}, u32[]{:S(2)}) collective-permute-start(s32[1]{0:T(128)} %param.15), channel_id=1, source_target_pairs={{10,0},{11,1},{12,2},{13,3},{14,4},{15,5},{0,6},{1,7},{2,8},{3,9},... | collective-permute-start | bytes 20 | tf_op jit(solution)/shard_map/ppermute | solution.py:14
  45.3 3.9 collective-permute-start.6
  49.8 38.7 %collective-permute-start.14 = (s32[2]{0:T(128)S(1)}, s32[2]{0:T(128)S(1)}, u32[]{:S(2)}, u32[]{:S(2)}) collective-permute-start(s32[2]{0:T(128)S(1)} %pad_add_fusion.2), channel_id=1, source_target_pairs={{4,0},{5,1},{6,2},{7,3},{8,4},{9,5},{10,6},{11,7},{12,8},{13,9},{1... | collective-permute-start | bytes 32 | tf_op jit(solution)/shard_map/ppermute | solution.py:14
  84.9 4.9 %collective-permute-start.10 = (s32[2]{0:T(128)S(1)}, s32[2]{0:T(128)S(1)}, u32[]{:S(2)}, u32[]{:S(2)}) collective-permute-start(s32[2]{0:T(128)S(1)} %pad_add_fusion.2), channel_id=1, source_target_pairs={{2,0},{3,1},{4,2},{5,3},{6,4},{7,5},{8,6},{9,7},{10,8},{11,9},{12,... | collective-permute-start | bytes 32 | tf_op jit(solution)/shard_map/ppermute | solution.py:14
  87.9 29.3 %copy-start.1 = (s32[1,16]{1,0:T(1,128)S(1)}, s32[1,16]{1,0:T(1,128)}, u32[]{:S(2)}) copy-start(s32[1,16]{1,0:T(1,128)} %param.17) | copy-start | bytes 196
  87.9 24.1 %collective-permute-start.7 = (f32[6,256,256]{2,1,0:T(8,128)S(1)}, f32[6,256,256]{2,1,0:T(8,128)S(1)}, u32[]{:S(2)}, u32[]{:S(2)}) collective-permute-start(f32[6,256,256]{2,1,0:T(8,128)S(1)} %broadcast_select_fusion), channel_id=1, source_target_pairs={{1,0},{2,1},{3,2},{4,3},{5,4},{6,5},{7,6},{8,7},{9,8},{10,9},{11,1... | collective-permute-start | bytes 4718600 | tf_op jit(solution)/shard_map/ppermute | solution.py:14
  92.3 16.5 %collective-permute-start.5 = (s32[6]{0:T(128)S(1)}, s32[6]{0:T(128)S(1)}, u32[]{:S(2)}, u32[]{:S(2)}) collective-permute-start(s32[6]{0:T(128)S(1)} %broadcast_select_fusion.1), channel_id=1, source_target_pairs={{1,0},{2,1},{3,2},{4,3},{5,4},{6,5},{7,6},{8,7},{9,8},{10,9},{11,1... | collective-permute-start | bytes 80 | tf_op jit(solution)/shard_map/ppermute | solution.py:14
  94.0 16.8 %collective-permute-start.4 = (s32[6]{0:T(128)S(1)}, s32[6]{0:T(128)S(1)}, u32[]{:S(2)}, u32[]{:S(2)}) collective-permute-start(s32[6]{0:T(128)S(1)} %broadcast_select_fusion.2), channel_id=1, source_target_pairs={{1,0},{2,1},{3,2},{4,3},{5,4},{6,5},{7,6},{8,7},{9,8},{10,9},{11,1... | collective-permute-start | bytes 80 | tf_op jit(solution)/shard_map/ppermute | solution.py:14
  108.9 7.1 %collective-permute-start.9 = (s32[12]{0:T(128)S(1)}, s32[12]{0:T(128)S(1)}, u32[]{:S(2)}, u32[]{:S(2)}) collective-permute-start(s32[12]{0:T(128)S(1)} %pad_add_fusion.1), channel_id=1, source_target_pairs={{2,0},{3,1},{4,2},{5,3},{6,4},{7,5},{8,6},{9,7},{10,8},{11,9},{12,... | collective-permute-start | bytes 152 | tf_op jit(solution)/shard_map/ppermute | solution.py:14
  109.2 7.7 %collective-permute-start.13 = (s32[12]{0:T(128)S(1)}, s32[12]{0:T(128)S(1)}, u32[]{:S(2)}, u32[]{:S(2)}) collective-permute-start(s32[12]{0:T(128)S(1)} %pad_add_fusion.1), channel_id=1, source_target_pairs={{4,0},{5,1},{6,2},{7,3},{8,4},{9,5},{10,6},{11,7},{12,8},{13,9},{1... | collective-permute-start | bytes 152 | tf_op jit(solution)/shard_map/ppermute | solution.py:14
  110.9 6.1 %collective-permute-start.12 = (s32[12]{0:T(128)S(1)}, s32[12]{0:T(128)S(1)}, u32[]{:S(2)}, u32[]{:S(2)}) collective-permute-start(s32[12]{0:T(128)S(1)} %pad_add_fusion), channel_id=1, source_target_pairs={{4,0},{5,1},{6,2},{7,3},{8,4},{9,5},{10,6},{11,7},{12,8},{13,9},{1... | collective-permute-start | bytes 152 | tf_op jit(solution)/shard_map/ppermute | solution.py:14
  110.9 6.1 %collective-permute-start.8 = (s32[12]{0:T(128)S(1)}, s32[12]{0:T(128)S(1)}, u32[]{:S(2)}, u32[]{:S(2)}) collective-permute-start(s32[12]{0:T(128)S(1)} %pad_add_fusion), channel_id=1, source_target_pairs={{2,0},{3,1},{4,2},{5,3},{6,4},{7,5},{8,6},{9,7},{10,8},{11,9},{12,... | collective-permute-start | bytes 152 | tf_op jit(solution)/shard_map/ppermute | solution.py:14
  114.0 69.8 %collective-permute-start.15 = (f32[12,256,256]{2,1,0:T(8,128)}, f32[12,256,256]{2,1,0:T(8,128)}, u32[]{:S(2)}, u32[]{:S(2)}) collective-permute-start(f32[12,256,256]{2,1,0:T(8,128)} %pad_maximum_fusion), channel_id=1, source_target_pairs={{4,0},{5,1},{6,2},{7,3},{8,4},{9,5},{10,6},{11,7},{12,8},{13,9},{1... | collective-permute-start | bytes 9437192 | tf_op jit(solution)/shard_map/ppermute | solution.py:14
  116.0 134.8 %collective-permute-start.11 = (f32[12,256,256]{2,1,0:T(8,128)}, f32[12,256,256]{2,1,0:T(8,128)}, u32[]{:S(2)}, u32[]{:S(2)}) collective-permute-start(f32[12,256,256]{2,1,0:T(8,128)} %pad_maximum_fusion), channel_id=1, source_target_pairs={{2,0},{3,1},{4,2},{5,3},{6,4},{7,5},{8,6},{9,7},{10,8},{11,9},{12,... | collective-permute-start | bytes 9437192 | tf_op jit(solution)/shard_map/ppermute | solution.py:14
  320.4 14.6 %slice-start.4 = ((s8[8388608]{0:T(1024)(128)(4,1)}), s8[4194304]{0:T(1024)(128)(4,1)S(1)}, s32[]{:S(2)}) async-start(s8[8388608]{0:T(1024)(128)(4,1)} %bitcast.165), calls=%async_computation.6 | async-start | bytes 8388608
  327.1 8.0 %slice-start.5 = ((s8[8388608]{0:T(1024)(128)(4,1)}), s8[4194304]{0:T(1024)(128)(4,1)S(1)}, s32[]{:S(2)}) async-start(s8[8388608]{0:T(1024)(128)(4,1)} %bitcast.165), calls=%async_computation.7 | async-start | bytes 8388608
  327.1 13.6 %slice-start.2 = ((s8[8388608]{0:T(1024)(128)(4,1)}), s8[4194304]{0:T(1024)(128)(4,1)S(1)}, s32[]{:S(2)}) async-start(s8[8388608]{0:T(1024)(128)(4,1)} %bitcast.163), calls=%async_computation.4 | async-start | bytes 8388608
  335.0 5.7 %slice-start.3 = ((s8[8388608]{0:T(1024)(128)(4,1)}), s8[4194304]{0:T(1024)(128)(4,1)S(1)}, s32[]{:S(2)}) async-start(s8[8388608]{0:T(1024)(128)(4,1)} %bitcast.163), calls=%async_computation.5 | async-start | bytes 8388608
  335.0 11.6 %slice-start = ((s8[8388608]{0:T(1024)(128)(4,1)}), s8[4194304]{0:T(1024)(128)(4,1)S(1)}, s32[]{:S(2)}) async-start(s8[8388608]{0:T(1024)(128)(4,1)} %bitcast.161), calls=%async_computation.2 | async-start | bytes 8388608
  340.7 5.9 %slice-start.1 = ((s8[8388608]{0:T(1024)(128)(4,1)}), s8[4194304]{0:T(1024)(128)(4,1)S(1)}, s32[]{:S(2)}) async-start(s8[8388608]{0:T(1024)(128)(4,1)} %bitcast.161), calls=%async_computation.3 | async-start | bytes 8388608
  340.7 5.9 %copy-start = (f32[16,256,256,1]{2,0,3,1:T(8,128)S(1)}, f32[16,256,256,1]{2,0,3,1:T(8,128)}, u32[]{:S(2)}) copy-start(f32[16,256,256,1]{2,0,3,1:T(8,128)} %fusion.8) | copy-start | bytes 12582916
  356.3 0.7 copy-start.2
Sparse Core Ops, SparseCore 0:
  356.5 56.4 reduce-scatter.1
where the time goes:
time: 430 us; the launch traced here: 424 us
  waiting for transfers between devices  156 us (36%)
  matrix products  125 us (29%)
  local copies, waits for them, and re-layouts  64 us (15%)
  starting transfers between devices  53.5 us (12%)
  between operations  15.3 us (4%)
  other arithmetic  10.4 us (2%)
    ppermute x16, waiting for transfers between devices, shifted(): return lax.ppermute(block, axis, route)  100 us
    dot_general x6, matrix products, contribute(): jnp.einsum('kij,qjl->kqil', a_group, blocks, precision=lax.Precision.HIGH...  80.9 us
    dot_general x6, local copies, waits for them, and re-layouts, contribute(): jnp.einsum('kij,qjl->kqil', a_group, blocks, precision=lax.Precision.HIGH...  57.9 us
    reduce_scatter x1, waiting for transfers between devices, local(): lax.psum_scatter(partial_sum, 'rep', scatter_dimension=0, tiled=True)  55.9 us
    ppermute x16, starting transfers between devices, shifted(): return lax.ppermute(block, axis, route)  53.5 us
    dot_general x6, matrix products, contribute(): jnp.einsum('tkq,kqil->til', weights.astype(jnp.float32), products, precis...  43.8 us
  transfers between devices with their start and end apart: 17, of which 6 were waited for; matrix products, arithmetic and copies ran while one was open for 21% of the time, Pallas kernels for 0%

commit v1 on v0

v1 whole, which is shorter than its diff:
```python
import functools

import jax
import jax.numpy as jnp
from jax import lax
from jax.experimental import pallas as pl
from jax.experimental.pallas import tpu as pltpu
from jax.sharding import PartitionSpec as P

STEPS = 6
A_SLOTS = 4
ROWS_DEV = 2
LANES = 128
MESH = pl.DeviceIdType.MESH


def kernel(
    n,
    a_rows,
    a_cols,
    c_rows,
    c_cols,
    meta_ref,
    a_ref,
    b_ref,
    out_ref,
    panels,
    metas,
    metas_s,
    a_vmem,
    a_split,
    prods,
    acc,
    far,
    local_sem,
    z_send,
    z_recv,
    x_send,
    x_recv,
    f_send,
    f_recv,
    s_send,
    s_recv,
    y_send,
    y_recv,
    m_send,
    m_recv,
):
    rep = lax.axis_index("rep")
    me = lax.axis_index("blk")
    core = lax.rem(me, 2)
    odd = lax.rem(me // 2, 2)
    slots = panels.shape[1]
    halves = panels.shape[2]
    q_count = panels.shape[3]
    block = panels.shape[4]
    targets = acc.shape[1]
    keep = targets // 2
    ahead = lax.rem(me + 4, n)
    behind = lax.rem(me + n - 4, n)
    z_to = jnp.where(rep == 0, ahead, behind)
    x_to = me + 2 - 4 * odd
    s_to = me + 1 - 2 * core
    near = jnp.where(rep == 0, odd, 1 - odd)

    barrier = pltpu.get_barrier_semaphore()
    for other in (ahead, behind, x_to, s_to):
        pl.semaphore_signal(barrier, inc=1, device_id=(rep, other), device_id_type=MESH)
    pl.semaphore_signal(barrier, inc=1, device_id=(1 - rep, me), device_id_type=MESH)
    pl.semaphore_wait(barrier, 5)

    def remote(src, dst, send, recv, to, r=None):
        return pltpu.make_async_remote_copy(
            src_ref=src,
            dst_ref=dst,
            send_sem=send,
            recv_sem=recv,
            device_id=(rep if r is None else r, to),
            device_id_type=MESH,
        )

    def own(h, q):
        return b_ref.at[q, :, pl.ds(h * LANES, LANES)]

    def z_copy(h, q):
        return remote(own(h, q), panels.at[0, 2, h, q], z_send.at[h, q], z_recv.at[h, q], z_to)

    def x_own(h, q):
        return remote(own(h, q), panels.at[0, 1, h, q], x_send.at[h, q], x_recv.at[h, q], x_to)

    def x_pass(h, q):
        return remote(
            panels.at[0, 2, h, q], panels.at[0, 1, h, q], x_send.at[h, q], x_recv.at[h, q], x_to
        )

    def f_copy(h, q):
        return remote(
            panels.at[0, 1, h, q], panels.at[0, 3, h, q], f_send.at[h, q], f_recv.at[h, q], z_to
        )

    def s_copy(s, h):
        return remote(panels.at[0, s, h], panels.at[1, s, h], s_send.at[s, h], s_recv.at[s, h], s_to)

    def meta_copy(index, src, line, slot, to):
        return remote(src, metas.at[line, slot], m_send.at[index], m_recv.at[index], to)

    def y_copy(h):
        return remote(
            acc.at[h, pl.ds((1 - rep) * keep, keep)],
            far.at[h],
            y_send.at[h],
            y_recv.at[h],
            me,
            1 - rep,
        )

    def start_own(h):
        for q in range(q_count):
            z_copy(h, q).start()

        @pl.when(near == 0)
        def _():
            for q in range(q_count):
                x_own(h, q).start()

    m_z = meta_copy(0, meta_ref, 0, 2, z_to)
    m_x = meta_copy(1, meta_ref, 0, 1, x_to)
    m_xp = meta_copy(1, metas.at[0, 2], 0, 1, x_to)
    m_f = meta_copy(2, metas.at[0, 1], 0, 3, z_to)
    m_s = [meta_copy(3 + s, metas.at[0, s], 1, s, s_to) for s in range(slots)]
    m_s[0] = meta_copy(3, meta_ref, 1, 0, s_to)

    m_z.start()

    @pl.when(near == 0)
    def _():
        m_x.start()

    m_s[0].start()
    start_own(0)
    mine = [
        pltpu.make_async_copy(
            b_ref.at[:, :, pl.ds(h * LANES, LANES)], panels.at[0, 0, h], local_sem.at[h]
        )
        for h in range(halves)
    ]
    for copy in mine:
        copy.start()
    a_copy = pltpu.make_async_copy(a_ref, a_vmem, local_sem.at[halves])
    a_copy.start()
    m_own = pltpu.make_async_copy(meta_ref, metas.at[0, 0], local_sem.at[halves + 1])
    m_own.start()
    for h in range(halves):
        mine[h].wait()
        s_copy(0, h).start()
    m_own.wait()

    m_z.wait_recv()

    @pl.when(near == 1)
    def _():
        m_xp.start()

    m_s[2].start()
    m_x.wait_recv()
    m_f.start()
    m_s[1].start()

    a_copy.wait()
    tile = 64

    def split_a(index, carry):
        k = index // (block // tile)
        rows = pl.ds(pl.multiple_of(lax.rem(index, block // tile) * tile, tile), tile)
        owner = lax.rem(me + (rep - 1) * STEPS + k + n, n)
        parts = [a_vmem[k * A_SLOTS + m, rows, :] for m in range(A_SLOTS)]
        for i in range(ROWS_DEV):
            for j in range(ROWS_DEV):
                total = None
                for m in range(A_SLOTS):
                    g = k * A_SLOTS + m
                    match = (a_rows[0, g] == me * ROWS_DEV + i) & (
                        a_cols[0, g] == owner * ROWS_DEV + j
                    )
                    term = jnp.where(match, 1.0, 0.0).astype(jnp.float32) * parts[m]
                    total = term if total is None else total + term
                high = total.astype(jnp.bfloat16)
                low = (total - high.astype(jnp.float32)).astype(jnp.bfloat16)
                a_split[k, j, i, rows, pl.ds(0, block)] = high
                a_split[k, j, i, rows, pl.ds(block, block)] = low
                a_split[k, j, i, rows, pl.ds(2 * block, block)] = high
        return carry

    lax.fori_loop(0, STEPS * (block // tile), split_a, 0)

    def clear(index, carry):
        h = index // targets
        t = lax.rem(index, targets)
        acc[h, t] = jnp.zeros((block, LANES), jnp.float32)
        return carry

    lax.fori_loop(0, halves * targets, clear, 0)

    m_f.wait_recv()
    m_s[3].start()
    for s in range(slots):
        m_s[s].wait_recv()
    m_scalar = pltpu.make_async_copy(metas, metas_s, local_sem.at[halves + 2])
    m_scalar.start()
    m_scalar.wait()

    def compute(line, slot, h):
        back = STEPS - 2 * slot + line * (1 - 2 * core)
        forth = 2 * slot + line * (1 - 2 * core)
        k = jnp.where(rep == 0, back, forth)

        @pl.when((k >= 0) & (k < STEPS))
        def _():
            def multiply(q, carry):
                piece = panels[line, slot, h, q]
                high = piece.astype(jnp.bfloat16)
                low = (piece - high.astype(jnp.float32)).astype(jnp.bfloat16)
                stacked = jnp.concatenate([high, high, low], axis=0)
                j = lax.rem(metas_s[line, slot, 0, q], ROWS_DEV)
                left = a_split[k, j].reshape(ROWS_DEV * block, 3 * block)
                product = jnp.dot(left, stacked, preferred_element_type=jnp.float32)
                prods[q] = product.reshape(ROWS_DEV, block, LANES)
                return carry

            lax.fori_loop(0, q_count, multiply, 0)

            def collect(t, carry):
                i = lax.rem(c_rows[0, t], ROWS_DEV)
                total = acc[h, t]
                for q in range(q_count):
                    match = metas_s[line, slot, 1, q] == c_cols[0, t]
                    total = total + jnp.where(match, 1.0, 0.0).astype(jnp.float32) * prods[q, i]
                acc[h, t] = total
                return carry

            lax.fori_loop(0, targets, collect, 0)

    for h in range(halves):
        compute(0, 0, h)
        s_copy(0, h).wait_recv()
        compute(1, 0, h)
        for q in range(q_count):
            z_copy(h, q).wait_recv()

            @pl.when(near == 1)
            def _():
                x_pass(h, q).start()

            x_own(h, q).wait_recv()
            f_copy(h, q).start()
        s_copy(2, h).start()
        s_copy(1, h).start()
        if h + 1 < halves:
            start_own(h + 1)
        compute(0, 2, h)
        compute(0, 1, h)
        s_copy(2, h).wait_recv()
        compute(1, 2, h)
        s_copy(1, h).wait_recv()
        compute(1, 1, h)
        for q in range(q_count):
            f_copy(h, q).wait_recv()
        s_copy(3, h).start()
        compute(0, 3, h)
        s_copy(3, h).wait_recv()
        compute(1, 3, h)
        y_copy(h).start()

    for h in range(halves):
        y_copy(h).wait_recv()

        def finish(t, carry):
            out_ref[t, :, pl.ds(h * LANES, LANES)] = acc[h, rep * keep + t] + far[h, t]
            return carry

        lax.fori_loop(0, keep, finish, 0)

    for copy in [m_z, m_x, m_f] + m_s:
        copy.wait_send()
    for h in range(halves):
        y_copy(h).wait_send()
        for s in range(slots):
            s_copy(s, h).wait_send()
        for q in range(q_count):
            z_copy(h, q).wait_send()
            x_own(h, q).wait_send()
            f_copy(h, q).wait_send()


def local(n, a_blocks, a_rows, a_cols, b_blocks, b_rows, b_cols, b_count, c_rows, c_cols):
    replica = lax.axis_index("rep")
    q_count, block = b_blocks.shape[1], b_blocks.shape[-1]
    a_slots = a_blocks.shape[1]
    targets = c_rows.shape[1]
    half = targets // lax.axis_size("rep")
    halves = block // LANES
    slots = STEPS // 2 + 1
    live = jnp.arange(q_count, dtype=jnp.int32) < b_count[0]
    cols = jnp.where(live, b_cols[0], -1)
    meta = jnp.pad(jnp.stack([b_rows[0], cols]), ((0, 6), (0, LANES - q_count)))
    smem = pl.BlockSpec(memory_space=pltpu.SMEM)
    vmem = pl.BlockSpec(memory_space=pltpu.VMEM)
    hbm = pl.BlockSpec(memory_space=pl.ANY)
    dma = pltpu.SemaphoreType.DMA
    summed = pl.pallas_call(
        functools.partial(kernel, n),
        out_shape=jax.ShapeDtypeStruct((half, block, block), jnp.float32),
        in_specs=[smem] * 4 + [vmem, hbm, hbm],
        out_specs=vmem,
        scratch_shapes=[
            pltpu.VMEM((2, slots, halves, q_count, block, LANES), jnp.float32),
            pltpu.VMEM((2, slots, 8, LANES), jnp.int32),
            pltpu.SMEM((2, slots, 8, LANES), jnp.int32),
            pltpu.VMEM((a_slots, block, block), jnp.float32),
            pltpu.VMEM((STEPS, ROWS_DEV, ROWS_DEV, block, 3 * block), jnp.bfloat16),
            pltpu.VMEM((q_count, ROWS_DEV, block, LANES), jnp.float32),
            pltpu.VMEM((halves, targets, block, LANES), jnp.float32),
            pltpu.VMEM((halves, half, block, LANES), jnp.float32),
            dma((halves + 3,)),
            dma((halves, q_count)),
            dma((halves, q_count)),
            dma((halves, q_count)),
            dma((halves, q_count)),
            dma((halves, q_count)),
            dma((halves, q_count)),
            dma((slots, halves)),
            dma((slots, halves)),
            dma((halves,)),
            dma((halves,)),
            dma((3 + slots,)),
            dma((3 + slots,)),
        ],
        compiler_params=pltpu.CompilerParams(
            collective_id=0, has_side_effects=True, vmem_limit_bytes=60 * 1024 * 1024
        ),
    )(a_rows, a_cols, c_rows, c_cols, meta, a_blocks[0], b_blocks[0])
    rows_half = lax.dynamic_slice_in_dim(c_rows[0], replica * half, half)
    cols_half = lax.dynamic_slice_in_dim(c_cols[0], replica * half, half)
    diagonal = (rows_half == cols_half).astype(jnp.float32)
    identity = jnp.eye(block, dtype=jnp.float32)
    result = 1.5 * diagonal[:, None, None] * identity[None, :, :] - 0.5 * summed
    return result[None]


def solution(mesh):
    return jax.shard_map(
        functools.partial(local, mesh.shape["blk"]),
        mesh=mesh,
        in_specs=(
            P("blk", "rep", None, None),
            P("blk", "rep"),
            P("blk", "rep"),
            P("blk", None, None, None),
            P("blk", None),
            P("blk", None),
            P("blk"),
            P("blk", None),
            P("blk", None),
        ),
        out_specs=P("blk", "rep", None, None),
        check_vma=False,
    )
```

time: 430 us -> 125 us (0.29); the launches traced: 424 us -> 124 us
  waiting for transfers between devices: 156 us -> 0 us
  matrix products: 125 us -> 0 us
  Pallas kernels: 0 us -> 117 us
  local copies, waits for them, and re-layouts: 64 us -> 0.6 us
  starting transfers between devices: 53.5 us -> 0 us
  between operations: 15.3 us -> 0.67 us
  other arithmetic: 10.4 us -> 5.32 us
    dot_general x12 -> x0, matrix products: 125 us -> none  [the longest x6 80.9 us: contribute(): jnp.einsum('kij,qjl->kqil', a_group, blocks, precision=lax.Precision.HIGH...]
    pallas_call x0 -> x1, Pallas kernels: none -> 117 us  [local(): pl.pallas_call(functools.partial(kernel, n), out_shape=jax.ShapeDtypeStru...]
    ppermute x16 -> x0, waiting for transfers between devices: 100 us -> none  [shifted(): return lax.ppermute(block, axis, route)]
    dot_general x6 -> x0, local copies, waits for them, and re-layouts: 57.9 us -> none  [contribute(): jnp.einsum('kij,qjl->kqil', a_group, blocks, precision=lax.Precision.HIGH...]
    reduce_scatter x1 -> x0, waiting for transfers between devices: 55.9 us -> none  [local(): lax.psum_scatter(partial_sum, 'rep', scatter_dimension=0, tiled=True)]
    ppermute x16 -> x0, starting transfers between devices: 53.5 us -> none  [shifted(): return lax.ppermute(block, axis, route)]
  transfers between devices with their start and end apart: 17 -> 0, of which waited for: 6 -> 0; matrix products, arithmetic and copies ran while one was open for 21% -> 0% of each run, Pallas kernels for 0% -> 0%
where the time goes in v1:
time: 125 us; the launch traced here: 124 us
  Pallas kernels  117 us (94%)
  other arithmetic  5.32 us (4%)
    pallas_call x1, Pallas kernels, local(): pl.pallas_call(functools.partial(kernel, n), out_shape=jax.ShapeDtypeStru...  117 us
    broadcast_in_dim x1, other arithmetic, local(): return result[None]  3.24 us

profile of v1, /device:TPU:3, one launch (start us, length us, event | category | flops | bytes accessed | tf_op | source)
XLA Modules:
  0.0 124.0 jit_solution(8296544147311935724)
XLA Ops:
  0.0 0.7 fusion.1
  1.4 0.7 compare_select_fusion
  2.1 0.7 pad_add_fusion
  2.7 0.6 pad.4.meta_ref
  3.3 117.4 %shard_map.91 = f32[8,256,256]{2,1,0:T(8,128)} custom-call(s32[1,24]{1,0:T(1,128)} %a_rows.1, s32[1,24]{1,0:T(1,128)} %a_cols.1, s32[1,16]{1,0:T(1,128)} %c_rows.1, s32[1,16]{1,0:T(1,128)} %c_cols.1, s32[8,128]{1,0:T(8,128)} %pad.4.meta_ref, f32[24,256,256]{2,1,0:T(8,128)} %bitcast.8, f32[6,256,256]{2,1,0:T(8,128)} %bitcast.9), custom_call_target="tpu_custom_call" | custom-call | tf_op jit(solution)/shard_map/pallas_call | solution.py:310
  120.7 3.2 %subtract_bitcast_fusion = f32[1,8,256,256]{3,2,1,0:T(8,128)} fusion(f32[8,256,256]{2,1,0:T(8,128)} %shard_map.91, f32[256,256]{1,0:T(8,128)S(1)} %fusion, f32[8]{0:T(128)S(1)} %fusion.1), kind=kLoop, calls=%fused_computation | loop fusion | flops 1572864 | bytes 4456480 | tf_op jit(solution)/shard_map/broadcast_in_dim | solution.py:347
  (1 shorter events, 0.0 us)

commit v2 on v1

--- a/solution.py
+++ b/solution.py
@@ -20,11 +20,14 @@
     a_cols,
     c_rows,
     c_cols,
-    meta_ref,
+    b_rows,
+    b_cols,
+    b_count,
     a_ref,
     b_ref,
     out_ref,
     panels,
+    detour,
     metas,
     metas_s,
     a_vmem,
@@ -41,6 +44,10 @@
     f_recv,
     s_send,
     s_recv,
+    p_send,
+    d_recv,
+    t_send,
+    t_recv,
     y_send,
     y_recv,
     m_send,
@@ -63,6 +70,15 @@
     s_to = me + 1 - 2 * core
     near = jnp.where(rep == 0, odd, 1 - odd)
 
+    sub = lax.broadcasted_iota(jnp.int32, (8, LANES), 0)
+    lane = lax.broadcasted_iota(jnp.int32, (8, LANES), 1)
+    meta = jnp.zeros((8, LANES), jnp.int32)
+    for q in range(q_count):
+        col = jnp.where(q < b_count[0], b_cols[0, q], -1)
+        meta = jnp.where((sub == 0) & (lane == q), b_rows[0, q], meta)
+        meta = jnp.where((sub == 1) & (lane == q), col, meta)
+    metas[0, 0] = meta
+
     barrier = pltpu.get_barrier_semaphore()
     for other in (ahead, behind, x_to, s_to):
         pl.semaphore_signal(barrier, inc=1, device_id=(rep, other), device_id_type=MESH)
@@ -98,18 +114,38 @@
             panels.at[0, 1, h, q], panels.at[0, 3, h, q], f_send.at[h, q], f_recv.at[h, q], z_to
         )
 
+    def p_copy(h, q):
+        return remote(
+            panels.at[0, 2, h, q], panels.at[0, 3, h, q], p_send.at[h, q], f_recv.at[h, q], x_to
+        )
+
+    def d_copy(h, q):
+        return remote(
+            panels.at[0, 2, h, q], detour.at[h, q], f_send.at[h, q], d_recv.at[h, q], z_to
+        )
+
+    def dp_copy(h, q):
+        return remote(
+            detour.at[h, q], panels.at[0, 3, h, q], p_send.at[h, q], f_recv.at[h, q], x_to
+        )
+
+    def t_copy(h, q):
+        return remote(
+            panels.at[0, 3, h, q], panels.at[1, 3, h, q], t_send.at[h, q], t_recv.at[h, q], s_to
+        )
+
     def s_copy(s, h):
         return remote(panels.at[0, s, h], panels.at[1, s, h], s_send.at[s, h], s_recv.at[s, h], s_to)
 
     def meta_copy(index, src, line, slot, to):
         return remote(src, metas.at[line, slot], m_send.at[index], m_recv.at[index], to)
 
-    def y_copy(h):
-        return remote(
-            acc.at[h, pl.ds((1 - rep) * keep, keep)],
-            far.at[h],
-            y_send.at[h],
-            y_recv.at[h],
+    def y_copy(h, u):
+        return remote(
+            acc.at[h, (1 - rep) * keep + u],
+            far.at[h, u],
+            y_send.at[h, u],
+            y_recv.at[h, u],
             me,
             1 - rep,
         )
@@ -123,12 +159,11 @@
             for q in range(q_count):
                 x_own(h, q).start()
 
-    m_z = meta_copy(0, meta_ref, 0, 2, z_to)
-    m_x = meta_copy(1, meta_ref, 0, 1, x_to)
+    m_z = meta_copy(0, metas.at[0, 0], 0, 2, z_to)
+    m_x = meta_copy(1, metas.at[0, 0], 0, 1, x_to)
     m_xp = meta_copy(1, metas.at[0, 2], 0, 1, x_to)
     m_f = meta_copy(2, metas.at[0, 1], 0, 3, z_to)
     m_s = [meta_copy(3 + s, metas.at[0, s], 1, s, s_to) for s in range(slots)]
-    m_s[0] = meta_copy(3, meta_ref, 1, 0, s_to)
 
     m_z.start()
 
@@ -148,12 +183,9 @@
         copy.start()
     a_copy = pltpu.make_async_copy(a_ref, a_vmem, local_sem.at[halves])
     a_copy.start()
-    m_own = pltpu.make_async_copy(meta_ref, metas.at[0, 0], local_sem.at[halves + 1])
-    m_own.start()
     for h in range(halves):
         mine[h].wait()
         s_copy(0, h).start()
-    m_own.wait()
 
     m_z.wait_recv()
 
@@ -169,9 +201,8 @@
     a_copy.wait()
     tile = 64
 
-    def split_a(index, carry):
-        k = index // (block // tile)
-        rows = pl.ds(pl.multiple_of(lax.rem(index, block // tile) * tile, tile), tile)
+    def split_a(k, index, carry):
+        rows = pl.ds(pl.multiple_of(index * tile, tile), tile)
         owner = lax.rem(me + (rep - 1) * STEPS + k + n, n)
         parts = [a_vmem[k * A_SLOTS + m, rows, :] for m in range(A_SLOTS)]
         for i in range(ROWS_DEV):
@@ -191,7 +222,8 @@
                 a_split[k, j, i, rows, pl.ds(2 * block, block)] = high
         return carry
 
-    lax.fori_loop(0, STEPS * (block // tile), split_a, 0)
+    for k in range(STEPS):
+        lax.fori_loop(0, block // tile, functools.partial(split_a, k), 0)
 
     def clear(index, carry):
         h = index // targets
@@ -205,77 +237,163 @@
     m_s[3].start()
     for s in range(slots):
         m_s[s].wait_recv()
-    m_scalar = pltpu.make_async_copy(metas, metas_s, local_sem.at[halves + 2])
+    m_scalar = pltpu.make_async_copy(metas, metas_s, local_sem.at[halves + 1])
     m_scalar.start()
     m_scalar.wait()
 
-    def compute(line, slot, h):
+    def step_of(line, slot):
         back = STEPS - 2 * slot + line * (1 - 2 * core)
         forth = 2 * slot + line * (1 - 2 * core)
         k = jnp.where(rep == 0, back, forth)
-
-        @pl.when((k >= 0) & (k < STEPS))
+        return k, (k >= 0) & (k < STEPS)
+
+    def multiply(line, slot, h, k, into, q):
+        piece = panels[line, slot, h, q]
+        high = piece.astype(jnp.bfloat16)
+        low = (piece - high.astype(jnp.float32)).astype(jnp.bfloat16)
+        stacked = jnp.concatenate([high, high, low], axis=0)
+        j = lax.rem(metas_s[line, slot, 0, q], ROWS_DEV)
+        left = a_split[k, j].reshape(ROWS_DEV * block, 3 * block)
+        product = jnp.dot(left, stacked, preferred_element_type=jnp.float32)
+        prods[into, q] = product.reshape(ROWS_DEV, block, LANES)
+
+    def multiply_if(line, slot, h, into, q):
+        k, needed = step_of(line, slot)
+
+        @pl.when(needed)
         def _():
-            def multiply(q, carry):
-                piece = panels[line, slot, h, q]
-                high = piece.astype(jnp.bfloat16)
-                low = (piece - high.astype(jnp.float32)).astype(jnp.bfloat16)
-                stacked = jnp.concatenate([high, high, low], axis=0)
-                j = lax.rem(metas_s[line, slot, 0, q], ROWS_DEV)
-                left = a_split[k, j].reshape(ROWS_DEV * block, 3 * block)
-                product = jnp.dot(left, stacked, preferred_element_type=jnp.float32)
-                prods[q] = product.reshape(ROWS_DEV, block, LANES)
+            multiply(line, slot, h, k, into, q)
+
+    def collect(line, slot, h, into, t):
+        i = lax.rem(c_rows[0, t], ROWS_DEV)
+        total = acc[h, t]
+        for q in range(q_count):
+            match = metas_s[line, slot, 1, q] == c_cols[0, t]
+            total = total + jnp.where(match, 1.0, 0.0).astype(jnp.float32) * prods[into, q, i]
+        acc[h, t] = total
+
+    def collect_all(line, slot, h, into):
+        k, needed = step_of(line, slot)
+
+        @pl.when(needed)
+        def _():
+            def body(t, carry):
+                collect(line, slot, h, into, t)
                 return carry
 
-            lax.fori_loop(0, q_count, multiply, 0)
-
-            def collect(t, carry):
-                i = lax.rem(c_rows[0, t], ROWS_DEV)
-                total = acc[h, t]
-                for q in range(q_count):
-                    match = metas_s[line, slot, 1, q] == c_cols[0, t]
-                    total = total + jnp.where(match, 1.0, 0.0).astype(jnp.float32) * prods[q, i]
-                acc[h, t] = total
+            lax.fori_loop(0, targets, body, 0)
+
+    def compute(line, slot, h):
+        k, needed = step_of(line, slot)
+
+        @pl.when(needed)
+        def _():
+            def body(q, carry):
+                multiply(line, slot, h, k, 0, q)
                 return carry
 
-            lax.fori_loop(0, targets, collect, 0)
+            lax.fori_loop(0, q_count, body, 0)
+
+        collect_all(line, slot, h, 0)
+
+    few = q_count // 3
+    many = 2 * few
 
     for h in range(halves):
-        compute(0, 0, h)
-        s_copy(0, h).wait_recv()
-        compute(1, 0, h)
+        if h > 0:
+            compute(0, 0, h)
+            s_copy(0, h).wait_recv()
+            compute(1, 0, h)
         for q in range(q_count):
             z_copy(h, q).wait_recv()
 
             @pl.when(near == 1)
             def _():
                 x_pass(h, q).start()
-
+                if q < few:
+                    d_copy(h, q).start()
+
+            if q < many:
+
+                @pl.when(near == 0)
+                def _():
+                    p_copy(h, q).start()
+
+            multiply_if(0, 2, h, 0, q)
             x_own(h, q).wait_recv()
-            f_copy(h, q).start()
+            if q >= many:
+                f_copy(h, q).start()
+            elif q >= few:
+
+                @pl.when(near == 0)
+                def _():
+                    f_copy(h, q).start()
+
+            multiply_if(0, 1, h, 1, q)
         s_copy(2, h).start()
         s_copy(1, h).start()
         if h + 1 < halves:
             start_own(h + 1)
-        compute(0, 2, h)
-        compute(0, 1, h)
+        collect_all(0, 2, h, 0)
+        collect_all(0, 1, h, 1)
         s_copy(2, h).wait_recv()
         compute(1, 2, h)
+
+        @pl.when(near == 1)
+        def _():
+            for q in range(few):
+                d_copy(h, q).wait_recv()
+                dp_copy(h, q).start()
+
         s_copy(1, h).wait_recv()
         compute(1, 1, h)
-        for q in range(q_count):
+        if h == 0:
+            compute(0, 0, h)
+            s_copy(0, h).wait_recv()
+            compute(1, 0, h)
+        order = list(range(few, many)) + list(range(few)) + list(range(many, q_count))
+        previous = None
+        for q in order:
             f_copy(h, q).wait_recv()
-        s_copy(3, h).start()
-        compute(0, 3, h)
-        s_copy(3, h).wait_recv()
-        compute(1, 3, h)
-        y_copy(h).start()
+            t_copy(h, q).start()
+            multiply_if(0, 3, h, 0, q)
+            if previous is not None:
+                t_copy(h, previous).wait_recv()
+                multiply_if(1, 3, h, 1, previous)
+            previous = q
+        t_copy(h, previous).wait_recv()
+        multiply_if(1, 3, h, 1, previous)
+
+        def last(base, t):
+            for line in range(2):
+                k, needed = step_of(line, 3)
+
+                @pl.when(needed)
+                def _():
+                    collect(line, 3, h, line, base + t)
+
+        def theirs(u, carry):
+            last((1 - rep) * keep, u)
+
+            @pl.when(u > 0)
+            def _():
+                y_copy(h, u - 1).start()
+
+            return carry
+
+        def ours(u, carry):
+            last(rep * keep, u)
+            return carry
+
+        lax.fori_loop(0, keep, theirs, 0)
+        y_copy(h, keep - 1).start()
+        lax.fori_loop(0, keep, ours, 0)
 
     for h in range(halves):
-        y_copy(h).wait_recv()
-
-        def finish(t, carry):
-            out_ref[t, :, pl.ds(h * LANES, LANES)] = acc[h, rep * keep + t] + far[h, t]
+
+        def finish(u, carry):
+            y_copy(h, u).wait_recv()
+            out_ref[u, :, pl.ds(h * LANES, LANES)] = acc[h, rep * keep + u] + far[h, u]
             return carry
 
         lax.fori_loop(0, keep, finish, 0)
@@ -283,13 +401,30 @@
     for copy in [m_z, m_x, m_f] + m_s:
         copy.wait_send()
     for h in range(halves):
-        y_copy(h).wait_send()
-        for s in range(slots):
+        for u in range(keep):
+            y_copy(h, u).wait_send()
+        for s in range(slots - 1):
             s_copy(s, h).wait_send()
         for q in range(q_count):
             z_copy(h, q).wait_send()
             x_own(h, q).wait_send()
-            f_copy(h, q).wait_send()
+            t_copy(h, q).wait_send()
+            if q < few:
+                p_copy(h, q).wait_send()
+
+                @pl.when(near == 1)
+                def _():
+                    d_copy(h, q).wait_send()
+
+            elif q < many:
+
+                @pl.when(near == 0)
+                def _():
+                    p_copy(h, q).wait_send()
+                    f_copy(h, q).wait_send()
+
+            else:
+                f_copy(h, q).wait_send()
 
 
 def local(n, a_blocks, a_rows, a_cols, b_blocks, b_rows, b_cols, b_count, c_rows, c_cols):
@@ -300,9 +435,6 @@
     half = targets // lax.axis_size("rep")
     halves = block // LANES
     slots = STEPS // 2 + 1
-    live = jnp.arange(q_count, dtype=jnp.int32) < b_count[0]
-    cols = jnp.where(live, b_cols[0], -1)
-    meta = jnp.pad(jnp.stack([b_rows[0], cols]), ((0, 6), (0, LANES - q_count)))
     smem = pl.BlockSpec(memory_space=pltpu.SMEM)
     vmem = pl.BlockSpec(memory_space=pltpu.VMEM)
     hbm = pl.BlockSpec(memory_space=pl.ANY)
@@ -310,18 +442,19 @@
     summed = pl.pallas_call(
         functools.partial(kernel, n),
         out_shape=jax.ShapeDtypeStruct((half, block, block), jnp.float32),
-        in_specs=[smem] * 4 + [vmem, hbm, hbm],
+        in_specs=[smem] * 7 + [hbm, hbm],
         out_specs=vmem,
         scratch_shapes=[
             pltpu.VMEM((2, slots, halves, q_count, block, LANES), jnp.float32),
+            pltpu.VMEM((halves, q_count // 3, block, LANES), jnp.float32),
             pltpu.VMEM((2, slots, 8, LANES), jnp.int32),
             pltpu.SMEM((2, slots, 8, LANES), jnp.int32),
             pltpu.VMEM((a_slots, block, block), jnp.float32),
             pltpu.VMEM((STEPS, ROWS_DEV, ROWS_DEV, block, 3 * block), jnp.bfloat16),
-            pltpu.VMEM((q_count, ROWS_DEV, block, LANES), jnp.float32),
+            pltpu.VMEM((2, q_count, ROWS_DEV, block, LANES), jnp.float32),
             pltpu.VMEM((halves, targets, block, LANES), jnp.float32),
             pltpu.VMEM((halves, half, block, LANES), jnp.float32),
-            dma((halves + 3,)),
+            dma((halves + 2,)),
             dma((halves, q_count)),
             dma((halves, q_count)),
             dma((halves, q_count)),
@@ -330,15 +463,19 @@
             dma((halves, q_count)),
             dma((slots, halves)),
             dma((slots, halves)),
-            dma((halves,)),
-            dma((halves,)),
+            dma((halves, q_count)),
+            dma((halves, q_count)),
+            dma((halves, q_count)),
+            dma((halves, q_count)),
+            dma((halves, half)),
+            dma((halves, half)),
             dma((3 + slots,)),
             dma((3 + slots,)),
         ],
         compiler_params=pltpu.CompilerParams(
             collective_id=0, has_side_effects=True, vmem_limit_bytes=60 * 1024 * 1024
         ),
-    )(a_rows, a_cols, c_rows, c_cols, meta, a_blocks[0], b_blocks[0])
+    )(a_rows, a_cols, c_rows, c_cols, b_rows, b_cols, b_count, a_blocks[0], b_blocks[0])
     rows_half = lax.dynamic_slice_in_dim(c_rows[0], replica * half, half)
     cols_half = lax.dynamic_slice_in_dim(c_cols[0], replica * half, half)
     diagonal = (rows_half == cols_half).astype(jnp.float32)

time: 125 us -> 120 us (0.960)
  Pallas kernels: 117 us -> 114 us
  other arithmetic: 5.32 us -> 4 us
    pallas_call x1, Pallas kernels: 117 us -> 114 us  [local(): pl.pallas_call(functools.partial(kernel, n), out_shape=jax.ShapeDtypeStru...]
where the time goes in v2:
time: 120 us; the launch traced here: 119 us
  Pallas kernels  114 us (95%)
  other arithmetic  4 us (3%)
    pallas_call x1, Pallas kernels, local(): pl.pallas_call(functools.partial(kernel, n), out_shape=jax.ShapeDtypeStru...  114 us
    broadcast_in_dim x1, other arithmetic, local(): return result[None]  3.24 us

profile of v2, /device:TPU:3, one launch (start us, length us, event | category | flops | bytes accessed | tf_op | source)
XLA Modules:
  0.0 118.8 jit_solution(6049488023380986077)
XLA Ops:
  0.0 0.7 fusion.1
  1.4 114.2 %shard_map.91 = f32[8,256,256]{2,1,0:T(8,128)} custom-call(s32[1,24]{1,0:T(1,128)} %a_rows.1, s32[1,24]{1,0:T(1,128)} %a_cols.1, s32[1,16]{1,0:T(1,128)} %c_rows.1, s32[1,16]{1,0:T(1,128)} %c_cols.1, s32[1,6]{1,0:T(1,128)} %b_rows.1, s32[1,6]{1,0:T(1,128)} %b_cols.1, s32[1]{0:T(128)S(6)} %copy.10.b_count, f32[24,256,256]{2,1,0:T(8,128)} %bitcast.6, ...), custom_call_target="tpu_custom_call" | custom-call | tf_op jit(solution)/shard_map/pallas_call | solution.py:442
  115.6 3.2 %subtract_bitcast_fusion = f32[1,8,256,256]{3,2,1,0:T(8,128)} fusion(f32[8,256,256]{2,1,0:T(8,128)} %shard_map.91, f32[256,256]{1,0:T(8,128)S(1)} %fusion, f32[8]{0:T(128)S(1)} %fusion.1), kind=kLoop, calls=%fused_computation | loop fusion | flops 1572864 | bytes 4456480 | tf_op jit(solution)/shard_map/broadcast_in_dim | solution.py:484
  (1 shorter events, 0.0 us)

commit v3 on v2

--- a/solution.py
+++ b/solution.py
@@ -187,17 +187,6 @@
         mine[h].wait()
         s_copy(0, h).start()
 
-    m_z.wait_recv()
-
-    @pl.when(near == 1)
-    def _():
-        m_xp.start()
-
-    m_s[2].start()
-    m_x.wait_recv()
-    m_f.start()
-    m_s[1].start()
-
     a_copy.wait()
     tile = 64
 
@@ -233,13 +222,14 @@
 
     lax.fori_loop(0, halves * targets, clear, 0)
 
-    m_f.wait_recv()
-    m_s[3].start()
-    for s in range(slots):
-        m_s[s].wait_recv()
-    m_scalar = pltpu.make_async_copy(metas, metas_s, local_sem.at[halves + 1])
-    m_scalar.start()
-    m_scalar.wait()
+    def fetch(first, count):
+        copy = pltpu.make_async_copy(
+            metas.at[:, pl.ds(first, count)],
+            metas_s.at[:, pl.ds(first, count)],
+            local_sem.at[halves + 1],
+        )
+        copy.start()
+        copy.wait()
 
     def step_of(line, slot):
         back = STEPS - 2 * slot + line * (1 - 2 * core)
@@ -289,22 +279,26 @@
         @pl.when(needed)
         def _():
             def body(q, carry):
-                multiply(line, slot, h, k, 0, q)
+                multiply(line, slot, h, k, 2, q)
                 return carry
 
             lax.fori_loop(0, q_count, body, 0)
 
-        collect_all(line, slot, h, 0)
+        collect_all(line, slot, h, 2)
 
     few = q_count // 3
     many = 2 * few
 
     for h in range(halves):
-        if h > 0:
-            compute(0, 0, h)
-            s_copy(0, h).wait_recv()
-            compute(1, 0, h)
         for q in range(q_count):
+            if h == 0 and q == 0:
+                m_z.wait_recv()
+
+                @pl.when(near == 1)
+                def _():
+                    m_xp.start()
+
+                m_s[2].start()
             z_copy(h, q).wait_recv()
 
             @pl.when(near == 1)
@@ -319,7 +313,8 @@
                 def _():
                     p_copy(h, q).start()
 
-            multiply_if(0, 2, h, 0, q)
+            if h > 0:
+                multiply_if(0, 2, h, 0, q)
             x_own(h, q).wait_recv()
             if q >= many:
                 f_copy(h, q).start()
@@ -329,13 +324,29 @@
                 def _():
                     f_copy(h, q).start()
 
-            multiply_if(0, 1, h, 1, q)
+            if h > 0:
+                multiply_if(0, 1, h, 1, q)
+                if q == q_count // 2:
+                    compute(0, 0, h)
+                    s_copy(0, h).wait_recv()
+                    compute(1, 0, h)
+            elif q == 0:
+                m_x.wait_recv()
+                m_f.start()
+                m_s[1].start()
         s_copy(2, h).start()
         s_copy(1, h).start()
         if h + 1 < halves:
             start_own(h + 1)
-        collect_all(0, 2, h, 0)
-        collect_all(0, 1, h, 1)
+        if h == 0:
+            for s in range(slots - 1):
+                m_s[s].wait_recv()
+            fetch(0, slots - 1)
+            compute(0, 2, h)
+            compute(0, 1, h)
+        else:
+            collect_all(0, 2, h, 0)
+            collect_all(0, 1, h, 1)
         s_copy(2, h).wait_recv()
         compute(1, 2, h)
 
@@ -351,6 +362,10 @@
             compute(0, 0, h)
             s_copy(0, h).wait_recv()
             compute(1, 0, h)
+            m_f.wait_recv()
+            m_s[3].start()
+            m_s[3].wait_recv()
+            fetch(slots - 1, 1)
         order = list(range(few, many)) + list(range(few)) + list(range(many, q_count))
         previous = None
         for q in order:
@@ -451,7 +466,7 @@
             pltpu.SMEM((2, slots, 8, LANES), jnp.int32),
             pltpu.VMEM((a_slots, block, block), jnp.float32),
             pltpu.VMEM((STEPS, ROWS_DEV, ROWS_DEV, block, 3 * block), jnp.bfloat16),
-            pltpu.VMEM((2, q_count, ROWS_DEV, block, LANES), jnp.float32),
+            pltpu.VMEM((3, q_count, ROWS_DEV, block, LANES), jnp.float32),
             pltpu.VMEM((halves, targets, block, LANES), jnp.float32),
             pltpu.VMEM((halves, half, block, LANES), jnp.float32),
             dma((halves + 2,)),

time: 120 us -> 118 us (0.983)
  no operation moved by 1% of the time
where the time goes in v3:
time: 118 us
  Pallas kernels  113 us (96%)
  other arithmetic  4 us (3%)
    pallas_call x1, Pallas kernels, local(): pl.pallas_call(functools.partial(kernel, n), out_shape=jax.ShapeDtypeStru...  113 us
    broadcast_in_dim x1, other arithmetic, local(): return result[None]  3.24 us

profile of v3, /device:TPU:3, one launch (start us, length us, event | category | flops | bytes accessed | tf_op | source)
XLA Modules:
  0.0 117.8 jit_solution(16675798762540470795)
XLA Ops:
  0.0 0.7 fusion.1
  1.4 113.1 %shard_map.91 = f32[8,256,256]{2,1,0:T(8,128)} custom-call(s32[1,24]{1,0:T(1,128)} %a_rows.1, s32[1,24]{1,0:T(1,128)} %a_cols.1, s32[1,16]{1,0:T(1,128)} %c_rows.1, s32[1,16]{1,0:T(1,128)} %c_cols.1, s32[1,6]{1,0:T(1,128)} %b_rows.1, s32[1,6]{1,0:T(1,128)} %b_cols.1, s32[1]{0:T(128)S(6)} %copy.10.b_count, f32[24,256,256]{2,1,0:T(8,128)} %bitcast.6, ...), custom_call_target="tpu_custom_call" | custom-call | tf_op jit(solution)/shard_map/pallas_call | solution.py:457
  114.6 3.2 %subtract_bitcast_fusion = f32[1,8,256,256]{3,2,1,0:T(8,128)} fusion(f32[8,256,256]{2,1,0:T(8,128)} %shard_map.91, f32[256,256]{1,0:T(8,128)S(1)} %fusion, f32[8]{0:T(128)S(1)} %fusion.1), kind=kLoop, calls=%fused_computation | loop fusion | flops 1572864 | bytes 4456480 | tf_op jit(solution)/shard_map/broadcast_in_dim | solution.py:499
  (1 shorter events, 0.0 us)

commit v4 on v3

--- a/solution.py
+++ b/solution.py
@@ -326,7 +326,7 @@
 
             if h > 0:
                 multiply_if(0, 1, h, 1, q)
-                if q == q_count // 2:
+                if q == q_count - 1:
                     compute(0, 0, h)
                     s_copy(0, h).wait_recv()
                     compute(1, 0, h)

time: 118 us -> 122 us (1.034)
  Pallas kernels: 113 us -> 117 us
    pallas_call x1, Pallas kernels: 113 us -> 117 us  [local(): pl.pallas_call(functools.partial(kernel, n), out_shape=jax.ShapeDtypeStru...]
where the time goes in v4:
time: 122 us
  Pallas kernels  117 us (96%)
  other arithmetic  4 us (3%)
    pallas_call x1, Pallas kernels, local(): pl.pallas_call(functools.partial(kernel, n), out_shape=jax.ShapeDtypeStru...  117 us
    broadcast_in_dim x1, other arithmetic, local(): return result[None]  3.24 us

profile of v4, /device:TPU:3, one launch (start us, length us, event | category | flops | bytes accessed | tf_op | source)
XLA Modules:
  0.0 121.9 jit_solution(11795527741322870070)
XLA Ops:
  0.0 0.7 fusion.1
  1.4 117.3 %shard_map.91 = f32[8,256,256]{2,1,0:T(8,128)} custom-call(s32[1,24]{1,0:T(1,128)} %a_rows.1, s32[1,24]{1,0:T(1,128)} %a_cols.1, s32[1,16]{1,0:T(1,128)} %c_rows.1, s32[1,16]{1,0:T(1,128)} %c_cols.1, s32[1,6]{1,0:T(1,128)} %b_rows.1, s32[1,6]{1,0:T(1,128)} %b_cols.1, s32[1]{0:T(128)S(6)} %copy.10.b_count, f32[24,256,256]{2,1,0:T(8,128)} %bitcast.6, ...), custom_call_target="tpu_custom_call" | custom-call | tf_op jit(solution)/shard_map/pallas_call | solution.py:457
  118.7 3.2 %subtract_bitcast_fusion = f32[1,8,256,256]{3,2,1,0:T(8,128)} fusion(f32[8,256,256]{2,1,0:T(8,128)} %shard_map.91, f32[256,256]{1,0:T(8,128)S(1)} %fusion, f32[8]{0:T(128)S(1)} %fusion.1), kind=kLoop, calls=%fused_computation | loop fusion | flops 1572864 | bytes 4456480 | tf_op jit(solution)/shard_map/broadcast_in_dim | solution.py:499
  (1 shorter events, 0.0 us)
